TPU v7x, 32 devices: a whole 2x2x4 slice. The times are simulated.
32 devices in a mesh: seq: 16 (over z, x, core), head: 2 (over y).
Axes of the slice: x: 2, y: 2, z: 4, core: 2. Of those that a mesh axis runs over, the one named last changes fastest.
Arguments:
- features: bfloat16 [8, 32, 8, 512], P(None, 'seq', 'head'), may hold values from -540 to 540
- gn_gain: float32 [512], replicated, may hold values from 0.5 to 1.5
- gn_bias: float32 [512], replicated, may hold values from -3 to 3
- conv_weight: bfloat16 [3, 3, 3, 16, 512], replicated, may hold values from -0.0546875 to 0.0546875
- conv_bias: float32 [16], replicated, may hold values from -3 to 3
- patch_weight: bfloat16 [64, 3072], replicated, may hold values from -0.75 to 0.75
- patch_bias: float32 [3072], replicated, may hold values from -3 to 3
- image_mod: float32 [3, 3072], replicated, may hold values from -3 to 3
- w_qkv: bfloat16 [3072, 3, 2048], P('seq', None, 'head'), may hold values from -5 to 5
- text_ids: int32 [512], replicated, may hold values from 0 to 16383
- text_length: int32 [1], replicated, may hold values from 256 to 512
- text_table: bfloat16 [3072, 16384], P('seq'), may hold values from -60 to 60
- text_mod: float32 [2, 3072], P(None, 'seq'), may hold values from -3 to 3
- w_text: bfloat16 [3072, 2, 2048], P('seq', None, 'head'), may hold values from -2 to 2
- w_out: bfloat16 [2048, 3072], P('head'), may hold values from -0.625 to 0.625
- out_bias: float32 [3072], replicated, may hold values from -3 to 3
Outputs:
- block_out: bfloat16 [8, 16, 4, 3072], P(None, 'seq', 'head')
All inputs are finite; a program needn't handle non-finite values.
Results may differ from a plain program's by a relative error of at most 0.0089.
Values may be sent and summed in bfloat16 or wider, within the bound.
A program may use at most 128 MiB of HBM per device.

v0:
```python
import jax
import jax.numpy as jnp
from jax import lax
from jax.sharding import PartitionSpec as P

HD = 128
GN_GROUPS = 32
CHUNK = 512
eps_norm = 1e-06


def group_gather(piece, group, dim):
    if group == 1:
        return piece
    count = lax.axis_size("seq")
    if group == 2:
        other = lax.ppermute(piece, "seq", [(i, i ^ 1) for i in range(count)])
        first = lax.axis_index("seq") % 2 == 0
        return jnp.concatenate(
            [jnp.where(first, piece, other), jnp.where(first, other, piece)], axis=dim
        )
    members = [list(range(i, i + group)) for i in range(0, count, group)]
    return lax.all_gather(piece, "seq", axis=dim, tiled=True, axis_index_groups=members)


def group_norm(features, gn_gain, gn_bias):
    frame_count, row_count, col_count, chan_count = features.shape
    per_group = chan_count // GN_GROUPS
    values = features.astype(jnp.float32)
    chan_sums = jnp.stack(
        [jnp.sum(values, axis=(0, 1, 2)), jnp.sum(values * values, axis=(0, 1, 2))]
    )
    sums = jnp.sum(chan_sums.reshape(2, GN_GROUPS, per_group), axis=2)
    sums = lax.psum(sums, ("seq", "head"))
    cell_count = (
        frame_count
        * row_count
        * col_count
        * per_group
        * lax.axis_size("seq")
        * lax.axis_size("head")
    )
    mean = sums[0] / cell_count
    scale = lax.rsqrt(sums[1] / cell_count - mean * mean + eps_norm)
    mean = jnp.repeat(mean, per_group)
    scale = jnp.repeat(scale, per_group)
    normed = (values - mean) * scale
    return jax.nn.silu(normed * gn_gain + gn_bias).astype(jnp.bfloat16)


def join_rims(parts, block_dim, dim, unit):
    size = parts.shape[dim]
    blocks = parts.shape[block_dim]
    core = lax.slice_in_dim(parts, unit, size - unit, axis=dim)
    low = lax.slice_in_dim(parts, 0, unit, axis=dim)
    high = lax.slice_in_dim(parts, size - unit, size, axis=dim)
    low = lax.slice_in_dim(low, 1, blocks, axis=block_dim)
    high = lax.slice_in_dim(high, 0, blocks - 1, axis=block_dim)
    pad_low = [(0, 0)] * parts.ndim
    pad_low[block_dim] = (0, 1)
    pad_low[dim] = (size - 3 * unit, 0)
    pad_high = [(0, 0)] * parts.ndim
    pad_high[block_dim] = (1, 0)
    pad_high[dim] = (0, size - 3 * unit)
    return core + jnp.pad(low, pad_low) + jnp.pad(high, pad_high)


def all_patches(activated, conv_weight, conv_bias):
    seq_n, head_n = (lax.axis_size("seq"), lax.axis_size("head"))
    frame_count, row_count, col_count, _ = activated.shape
    chans = conv_weight.shape[3]
    padded = jnp.concatenate([activated[:1], activated[:1], activated], axis=0)
    shares = lax.conv_general_dilated(
        padded[None],
        conv_weight,
        (1, 1, 1),
        ((0, 0), (2, 2), (2, 2)),
        dimension_numbers=("NDHWC", "DHWOI", "NDHWC"),
        preferred_element_type=jnp.float32,
    )[0]
    flat = shares.reshape(-1, 128)
    parts = lax.all_gather(flat, ("seq", "head"), axis=0, tiled=False)
    parts = parts.reshape(seq_n, head_n, frame_count, row_count + 2, (col_count + 2) * chans)
    parts = join_rims(join_rims(parts, 0, 3, 1), 1, 4, chans)
    latent = (parts + jnp.tile(conv_bias, col_count)).astype(jnp.bfloat16)
    blocks = latent.reshape(
        seq_n, head_n, frame_count, row_count // 2, 2, col_count // 2, 2 * chans
    )
    blocks = blocks.transpose(0, 1, 2, 3, 5, 4, 6)
    own = frame_count * (row_count // 2) * (col_count // 2)
    return blocks.reshape(seq_n * head_n * own, 4 * chans)


def modulate(patches, patch_weight, patch_bias, image_mod):
    hidden = jnp.dot(patches, patch_weight, preferred_element_type=jnp.float32) + patch_bias
    center = jnp.mean(hidden, axis=1, keepdims=True)
    offset = hidden - center
    spread = jnp.mean(offset * offset, axis=1, keepdims=True)
    normed = offset * lax.rsqrt(spread + eps_norm)
    return (normed * (1.0 + image_mod[1]) + image_mod[0]).astype(jnp.bfloat16)


def body(
    features,
    gn_gain,
    gn_bias,
    conv_weight,
    conv_bias,
    patch_weight,
    patch_bias,
    image_mod,
    w_qkv,
    text_ids,
    text_length,
    text_table,
    text_mod,
    w_text,
    w_out,
    out_bias,
):
    frame_count, row_count, col_count, _ = features.shape
    width_full = patch_weight.shape[1]
    seq_n, head_n = (lax.axis_size("seq"), lax.axis_size("head"))
    seq_i, head_i = (lax.axis_index("seq"), lax.axis_index("head"))
    depth, _, head_width = w_qkv.shape
    heads_here = head_width // HD
    group = seq_n // heads_here
    cols = head_width // seq_n
    text_count = text_ids.shape[0]
    both = jnp.concatenate([w_qkv, w_text], axis=1).reshape(depth, 5, seq_n, cols)
    both = both.transpose(2, 0, 1, 3).reshape(seq_n, depth, 5 * cols)
    both = lax.all_to_all(both, "seq", split_axis=0, concat_axis=0, tiled=True)
    both = both.reshape(seq_n * depth, 5, cols)
    both = group_gather(both, group, 2)
    w_query, w_image, w_text_full = (both[:, 0], both[:, 1:3], both[:, 3:5])
    chosen = (
        lax.broadcasted_iota(jnp.int32, (text_table.shape[1], text_count), 0) == text_ids[None, :]
    ).astype(jnp.bfloat16)
    own_context = jnp.dot(text_table, chosen, preferred_element_type=jnp.float32).astype(
        jnp.bfloat16
    )
    context = lax.all_gather(own_context, "seq", axis=0, tiled=True).astype(jnp.float32)
    mod = lax.all_gather(text_mod, "seq", axis=1, tiled=True)
    text_mean = jnp.sum(context, axis=0) / width_full
    text_square = jnp.sum(context * context, axis=0) / width_full
    text_scale = lax.rsqrt(text_square - text_mean * text_mean + eps_norm)
    text_normed = (context - text_mean) * text_scale * (1.0 + mod[1][:, None]) + mod[0][:, None]
    text_high = text_normed.astype(jnp.bfloat16)
    text_low = (text_normed - text_high.astype(jnp.float32)).astype(jnp.bfloat16)
    w_text_flat = w_text_full.reshape(width_full, 2 * HD)
    text_kv = sum(
        (
            lax.dot_general(
                part, w_text_flat, (((0,), (0,)), ((), ())), preferred_element_type=jnp.float32
            )
            for part in (text_high, text_low)
        )
    ).astype(jnp.bfloat16)
    activated = group_norm(features, gn_gain, gn_bias)
    patches = all_patches(activated, conv_weight, conv_bias)
    own = patches.shape[0] // (seq_n * head_n)
    part_rows = head_n * own // group
    my_part = seq_i % group
    chunk = min(CHUNK, patches.shape[0])

    def project(rows):
        modulated = modulate(rows, patch_weight, patch_bias, image_mod)
        kv = jnp.dot(
            modulated, w_image.reshape(width_full, 2 * HD), preferred_element_type=jnp.float32
        )
        query = jnp.dot(modulated, w_query, preferred_element_type=jnp.float32)
        query = lax.dynamic_index_in_dim(
            query.reshape(-1, group, part_rows, HD), my_part, axis=1, keepdims=False
        )
        return (kv.astype(jnp.bfloat16), query.reshape(-1, HD).astype(jnp.bfloat16))

    if chunk == patches.shape[0]:
        image_kv, query = project(patches)
    else:
        image_kv, query = lax.map(project, patches.reshape(-1, chunk, patches.shape[1]))
        image_kv = image_kv.reshape(-1, 2 * HD)
        query = query.reshape(-1, HD)
    keys = jnp.concatenate([image_kv[:, :HD], text_kv[:, :HD]], axis=0)
    vals = jnp.concatenate([image_kv[:, HD:], text_kv[:, HD:]], axis=0)
    key_valid = jnp.arange(keys.shape[0], dtype=jnp.int32) < image_kv.shape[0] + text_length[0]
    scores = (
        lax.dot_general(query, keys, (((1,), (1,)), ((), ())), preferred_element_type=jnp.float32)
        / HD
    )
    scores = jnp.where(key_valid[None, :], scores, -1e30)
    probs = jnp.exp(scores - jnp.max(scores, axis=1, keepdims=True))
    totals = jnp.sum(probs, axis=1, keepdims=True)
    attended = (
        jnp.dot(probs.astype(jnp.bfloat16), vals, preferred_element_type=jnp.float32) / totals
    ).astype(jnp.bfloat16)
    attended = attended.reshape(seq_n, part_rows, HD)
    attended = lax.all_to_all(attended, "seq", split_axis=0, concat_axis=0, tiled=True)
    attended = attended.reshape(heads_here, group, part_rows, HD).transpose(1, 2, 0, 3)
    attended = attended.reshape(head_n * own, head_width)
    if head_n == 2:
        halves = attended.reshape(2, own, head_width)
        away = jnp.dot(
            lax.dynamic_index_in_dim(halves, 1 - head_i, 0, keepdims=False),
            w_out,
            preferred_element_type=jnp.float32,
        )
        here = jnp.dot(
            lax.dynamic_index_in_dim(halves, head_i, 0, keepdims=False),
            w_out,
            preferred_element_type=jnp.float32,
        )
        projected = here + lax.ppermute(away, "head", [(0, 1), (1, 0)]) + out_bias
    else:
        projected = (
            lax.psum_scatter(
                jnp.dot(attended, w_out, preferred_element_type=jnp.float32),
                "head",
                scatter_dimension=0,
                tiled=True,
            )
            + out_bias
        )
    own_patches = lax.dynamic_slice_in_dim(patches, (seq_i * head_n + head_i) * own, own, axis=0)
    hidden = jnp.dot(own_patches, patch_weight, preferred_element_type=jnp.float32) + patch_bias
    block_out = (hidden + image_mod[2] * projected).astype(jnp.bfloat16)
    return block_out.reshape(frame_count, row_count // 2, col_count // 2, width_full)


def solution(mesh):
    return jax.shard_map(
        body,
        mesh=mesh,
        in_specs=(
            P(None, "seq", "head", None),
            P(),
            P(),
            P(),
            P(),
            P(),
            P(),
            P(),
            P("seq", None, "head"),
            P(),
            P(),
            P("seq", None),
            P(None, "seq"),
            P("seq", None, "head"),
            P("head", None),
            P(),
        ),
        out_specs=P(None, "seq", "head", None),
        check_vma=False,
    )
```

profile of v0, /device:TPU:0, one launch (start us, length us, event | category | flops | bytes accessed | tf_op | source)
XLA Modules:
  0.0 296.0 jit_solution(9451545067675089896)
XLA Ops:
  6.5 2.5 copy.83
  9.0 1.6 copy.82
  10.7 0.4 pad_maximum_fusion
  11.1 0.2 copy.84
  11.3 2.6 copy.85
  13.9 7.4 %all-to-all-start = ((bf16[16,192,320]{2,1,0:T(8,128)(2,1)}), bf16[16,192,320]{2,1,0:T(8,128)(2,1)}, u32[]{:S(2)}, u32[]{:S(2)}) async-start(bf16[16,192,320]{2,1,0:T(8,128)(2,1)} %copy.85), calls=%async_computation | async-start | bytes 4718592 | tf_op jit(solution)/shard_map/all_to_all | solution.py:132
  21.4 0.0 all-gather.3.cloned.1.call-start
  21.5 9.1 %fusion.23 = bf16[192,512]{1,0:T(8,128)(2,1)} fusion(bf16[192,16384]{1,0:T(8,128)(2,1)} %param.27, s32[512]{0:T(512)S(1)} %copy-done.19), kind=kOutput, calls=%fused_computation.34 | convolution fusion | flops 3229712384 | bytes 6490112 | tf_op jit(solution)/shard_map/dot_general | solution.py:139
  30.6 0.0 all-gather.3.cloned.1.call-update
  30.6 0.1 convert_reduce_fusion.1
  30.7 0.1 stack.10
  30.8 0.1 stack.9
  30.9 0.1 maximum_reduce_fusion
  31.0 83.9 %psum.7 = f32[2,32]{1,0:T(2,128)S(1)} all-reduce(f32[2,32]{1,0:T(2,128)S(1)} %maximum_reduce_fusion), channel_id=1, replica_groups=mesh['seq'=16,'head'=2] {'seq','head'}, use_global_device_ids=true, to_apply=%region_3.4 | all-reduce | flops 64 | bytes 512 | tf_op jit(solution)/shard_map/psum | solution.py:34
  114.8 0.1 broadcast_in_dim.15
  114.9 0.1 mul.93
  115.0 0.1 broadcast_in_dim.14
  115.1 0.1 sub.50
  115.2 0.1 fusion.50
  115.3 0.1 maximum_bitcast_fusion.2
  115.4 4.2 %convolution_reduce_fusion = f32[8,4,6,16]{3,2,1,0:T(8,128)S(1)} fusion(bf16[3,3,3,16,512]{4,3,2,1,0:T(8,128)(2,1)S(1)} %copy-done, bf16[1,10,2,4,512]{4,3,2,1,0:T(4,128)(2,1)S(1)} %maximum_bitcast_fusion.2), kind=kOutput, calls=%fused_computation.36 | convolution fusion | flops 28311552 | bytes 536576 | tf_op jit(solution)/shard_map/conv_general_dilated | solution.py:73
  119.6 0.1 all_gather_reshape_squeeze.3
  119.7 68.1 %all_gather.9 = f32[32,24,128]{2,1,0:T(8,128)S(1)} all-gather(f32[1,24,128]{2,1,0:T(8,128)S(1)} %all_gather_reshape_squeeze.3), channel_id=1, replica_groups=mesh['seq'=16,'head'=2] {'seq','head'}, dimensions={0}, use_global_device_ids=true | all-gather | bytes 405504 | tf_op jit(solution)/shard_map/all_gather | solution.py:82
  187.9 0.3 reshape.98
  188.2 0.1 slice.94
  188.4 0.1 add.179
  188.4 0.2 fusion.65
  188.7 0.1 fusion.68
  188.8 0.2 fusion.34
  189.0 0.1 reshape.99
  189.1 0.3 copy.81
  189.4 0.1 reshape.100
  189.6 3.6 %add_reduce_fusion = (f32[512]{0:T(512)S(1)}, f32[512,3072]{1,0:T(8,128)}) fusion(f32[3072]{0:T(1024)S(1)} %copy-done.11, bf16[512,64]{1,0:T(8,128)(2,1)S(1)} %reshape.100, bf16[64,3072]{1,0:T(8,128)(2,1)S(1)} %copy-done.7), kind=kOutput, calls=%fused_computation.15 | convolution fusion | flops 204471808 | bytes 6764544 | tf_op jit(solution)/shard_map/dot_general | solution.py:95
  193.2 17.4 %all-gather = f32[16,192,2]{1,2,0:T(2,128)S(1)} all-gather(f32[1,192,2]{1,2,0:T(2,128)S(1)} %bitcast.101), channel_id=1, replica_groups=mesh['seq'=16,'head'=2] {'seq'}, dimensions={0}, use_global_device_ids=true | all-gather | bytes 26112 | tf_op jit(solution)/shard_map/all_gather | solution.py:143
  210.6 0.1 reshape.110
  210.8 3.9 %copy.86 = bf16[16,192,320]{1,0,2:T(8,128)(2,1)S(1)} copy(bf16[16,192,320]{2,1,0:T(8,128)(2,1)} %all-to-all-done) | data formatting | bytes 3932160 | tf_op jit(solution)/shard_map/all_to_all | solution.py:132
  214.7 3.7 %reshape.103 = bf16[3072,5,64]{0,2,1:T(8,128)(2,1)} reshape(bf16[16,192,320]{1,0,2:T(8,128)(2,1)S(1)} %copy.86) | data formatting | bytes 3932160 | tf_op jit(solution)/shard_map/reshape | solution.py:133
  218.4 0.3 collective-permute-start
  218.7 3.7 %multiply_reduce_fusion = f32[512]{0:T(512)S(1)} fusion(f32[512,3072]{1,0:T(8,128)} %get-tuple-element.29, f32[512]{0:T(512)S(1)} %broadcast_multiply_fusion.1, f32[3072]{0:T(1024)S(1)} %copy-done.11), kind=kLoop, calls=%fused_computation.14 | loop fusion | flops 6290944 | bytes 6307840 | tf_op jit(solution)/shard_map/reduce_sum | solution.py:98
  223.2 6.3 %add_convert_fusion = bf16[512,3072]{1,0:T(8,128)(2,1)} fusion(f32[512,3072]{1,0:T(8,128)} %get-tuple-element.29, f32[3072]{0:T(1024)S(1)} %bitcast.95, f32[3072]{0:T(1024)S(1)} %bitcast.96, f32[512]{0:T(512)S(1)} %add_rsqrt_fusion.1, f32[512]{0:T(512)S(1)} %broadcast_multiply_fusion.1, f32[3072]{0:T(1024)S(1)} %copy-done.11), kind=kLoop, calls=%fused_computation.13 | loop fusion | flops 9437184 | bytes 9478144 | tf_op jit(solution)/shard_map/convert_element_type | solution.py:100
  229.5 3.1 %copy.87 = bf16[3072,5,64]{2,0,1:T(8,128)(2,1)} copy(bf16[3072,5,64]{0,2,1:T(8,128)(2,1)S(1)} %copy-done.5) | data formatting | bytes 3932160 | tf_op jit(solution)/shard_map/reshape | solution.py:133
  232.6 4.7 %copy.88 = bf16[3072,5,64]{2,0,1:T(8,128)(2,1)} copy(bf16[3072,5,64]{0,2,1:T(8,128)(2,1)} %collective-permute-done) | data formatting | bytes 3932160 | tf_op jit(solution)/shard_map/ppermute | solution.py:17
  237.3 3.6 %broadcast_select_fusion.1 = (bf16[3072,5,64]{2,0,1:T(8,128)(2,1)S(1)}, bf16[3072,5,64]{2,0,1:T(8,128)(2,1)S(1)}) fusion(bf16[3072,5,64]{2,0,1:T(8,128)(2,1)} %copy.87, bf16[3072,5,64]{2,0,1:T(8,128)(2,1)} %copy.88, pred[]{:T(512)S(6)} %eq.14), kind=kLoop, calls=%fused_computation.17 | loop fusion | flops 1966080 | bytes 7864321 | tf_op jit(solution)/shard_map/jit(_where)/select_n | solution.py:20
  240.9 3.3 %pad_maximum_fusion.2 = (bf16[3072,2,128]{2,0,1:T(8,128)(2,1)S(1)}, bf16[3072,2,128]{2,0,1:T(8,128)(2,1)}) fusion(bf16[3072,5,64]{2,0,1:T(8,128)(2,1)S(1)} %get-tuple-element.12, bf16[3072,5,64]{2,0,1:T(8,128)(2,1)S(1)} %get-tuple-element.11), kind=kLoop, calls=%fused_computation.27 | loop fusion | flops 6291456 | bytes 7077888 | tf_op jit(solution)/shard_map/slice | solution.py:135
  244.3 0.2 copy-done.3
  244.4 2.6 copy.93
  247.0 1.6 copy.91
  248.6 3.5 %fusion.27 = bf16[16,2,16,128]{3,2,1,0:T(8,128)(2,1)S(1)} fusion(bf16[16,2,16,3072]{3,2,1,0:T(8,128)(2,1)} %bitcast.80, bf16[3072,5,64]{2,0,1:T(8,128)(2,1)} %copy-done.3, bf16[3072,5,64]{2,0,1:T(8,128)(2,1)} %copy-done.2), kind=kOutput, calls=%fused_computation.42 | convolution fusion | flops 404226048 | bytes 7208960 | tf_op jit(solution)/shard_map/dot_general | solution.py:171
  252.2 0.2 copy-done.9
  252.4 1.0 convolution_convert_fusion
  253.4 0.0 all-gather.3.cloned.1.call-done
  253.5 2.8 convert_reduce_fusion
  256.2 4.0 %fusion.43 = f32[512,256]{1,0:T(8,128)S(1)} fusion(bf16[3072,256]{0,1:T(8,128)(2,1)S(1)} %bitcast.83, bf16[3072,512]{1,0:T(8,128)(2,1)} %all-gather.3.cloned.1.call-done, f32[3072]{0:T(1024)S(1)} %bitcast.99, f32[3072]{0:T(1024)S(1)} %bitcast.97, f32[512]{0:T(512)S(1)} %get-tuple-element.27, f32[512]{0:T(512)S(1)} %get-tuple-element.26), kind=kOutput, calls=%fused_computation.58 | convolution fusion | flops 814743552 | bytes 5271552 | tf_op jit(solution)/shard_map/dot_general | solution.py:153
  260.3 2.1 fusion.19
  262.4 0.4 fusion.70
  262.8 0.3 fusion.25
  263.1 1.0 fusion.24
  264.1 3.6 %all-to-all-start.1 = ((bf16[16,16,128]{2,1,0:T(8,128)(2,1)}), bf16[16,16,128]{2,1,0:T(8,128)(2,1)S(1)}, u32[]{:S(2)}, u32[]{:S(2)}) async-start(bf16[16,16,128]{2,1,0:T(8,128)(2,1)} %bitcast.24), calls=%async_computation.1 | async-start | bytes 131072 | tf_op jit(solution)/shard_map/all_to_all | solution.py:197
  267.7 6.8 %all-to-all-done.1 = bf16[16,16,128]{2,1,0:T(8,128)(2,1)S(1)} async-done(((bf16[16,16,128]{2,1,0:T(8,128)(2,1)}), bf16[16,16,128]{2,1,0:T(8,128)(2,1)S(1)}, u32[]{:S(2)}, u32[]{:S(2)}) %all-to-all-start.1) | async-done | bytes 65568 | tf_op jit(solution)/shard_map/all_to_all | solution.py:197
  274.6 3.8 %fusion.51 = f32[16,3072]{1,0:T(8,128)S(1)} fusion(bf16[1024,3072]{1,0:T(8,128)(2,1)} %param.30, bf16[2,16,1024]{2,1,0:T(8,128)(2,1)S(1)} %bitcast.89, s32[]{:T(128)S(6)} %select_n.47), kind=kOutput, calls=%fused_computation.73 | convolution fusion | flops 100663296 | bytes 6520836 | tf_op jit(solution)/shard_map/dot_general | solution.py:202
  278.4 0.9 convolution_add_fusion
  279.2 5.5 %collective-permute-done.1 = f32[16,3072]{1,0:T(8,128)S(1)} collective-permute-done((f32[16,3072]{1,0:T(8,128)S(1)}, f32[16,3072]{1,0:T(8,128)S(1)}, u32[]{:S(2)}, u32[]{:S(2)}) %collective-permute-start.1) | collective-permute-done | bytes 196640 | tf_op jit(solution)/shard_map/ppermute | solution.py:212
  284.8 3.7 %fusion.12 = bf16[16,3072]{1,0:T(8,128)(2,1)S(1)} fusion(f32[16,3072]{1,0:T(8,128)S(1)} %convolution_add_fusion, f32[16,3072]{1,0:T(8,128)S(1)} %collective-permute-done.1, bf16[1024,3072]{1,0:T(8,128)(2,1)} %param.30, f32[3072]{0:T(1024)S(1)} %copy-done.14, f32[3072]{0:T(1024)S(1)} %bitcast.94, bf16[2,16,1024]{2,1,0:T(8,128)(2,1)S(1)} %bitcast.90, ...), kind=kOutput, calls=%fused_computation.23 | convolution fusion | flops 100909056 | bytes 6840324 | tf_op jit(solution)/shard_map/dot_general | solution.py:207
  288.5 0.7 reshape.108
  (57 shorter events, 0.3 us)
Async XLA Ops:
  6.5 108.8 %copy-start = (bf16[3,3,3,16,512]{4,3,2,1,0:T(8,128)(2,1)S(1)}, bf16[3,3,3,16,512]{4,3,2,1,0:T(8,128)(2,1)}, u32[]{:S(2)}) copy-start(bf16[3,3,3,16,512]{4,3,2,1,0:T(8,128)(2,1)} %param.19) | copy-start | bytes 1327108
  11.3 10.1 %copy-start.19 = (s32[512]{0:T(512)S(1)}, s32[512]{0:T(512)}, u32[]{:S(2)}) copy-start(s32[512]{0:T(512)} %param.25) | copy-start | bytes 6148
  13.9 196.8 %all-to-all-start = ((bf16[16,192,320]{2,1,0:T(8,128)(2,1)}), bf16[16,192,320]{2,1,0:T(8,128)(2,1)}, u32[]{:S(2)}, u32[]{:S(2)}) async-start(bf16[16,192,320]{2,1,0:T(8,128)(2,1)} %copy.85), calls=%async_computation | async-start | bytes 4718592 | tf_op jit(solution)/shard_map/all_to_all | solution.py:132
  21.4 9.3 %copy-start.12 = (bf16[8,2,4,512]{3,2,1,0:T(4,128)(2,1)S(1)}, bf16[8,2,4,512]{3,2,1,0:T(4,128)(2,1)}, u32[]{:S(2)}) copy-start(bf16[8,2,4,512]{3,2,1,0:T(4,128)(2,1)} %param.16) | copy-start | bytes 196612
  21.4 93.8 %copy-start.15 = (f32[512]{0:T(512)S(1)}, f32[512]{0:T(512)}, u32[]{:S(2)}) copy-start(f32[512]{0:T(512)} %param.18) | copy-start | bytes 6148
  21.4 93.8 %copy-start.16 = (f32[512]{0:T(512)S(1)}, f32[512]{0:T(512)}, u32[]{:S(2)}) copy-start(f32[512]{0:T(512)} %param.17) | copy-start | bytes 6148
  21.4 167.0 %copy-start.18 = (f32[16]{0:T(128)S(1)}, f32[16]{0:T(128)}, u32[]{:S(2)}) copy-start(f32[16]{0:T(128)} %param.20) | copy-start | bytes 196
  21.4 232.0 %all-gather.3.cloned.1.call-start = ((), (), s32[]{:S(2)}) async-start(), calls=%async_computation.2 | async-start | bytes 3342336 | tf_op jit(solution)/shard_map/all_gather | solution.py:142
  30.6 158.9 %copy-start.7 = (bf16[64,3072]{1,0:T(8,128)(2,1)S(1)}, bf16[64,3072]{1,0:T(8,128)(2,1)}, u32[]{:S(2)}) copy-start(bf16[64,3072]{1,0:T(8,128)(2,1)} %param.21) | copy-start | bytes 1179652
  30.6 158.9 %copy-start.11 = (f32[3072]{0:T(1024)S(1)}, f32[3072]{0:T(1024)}, u32[]{:S(2)}) copy-start(f32[3072]{0:T(1024)} %param.22) | copy-start | bytes 36868
  189.5 3.7 %copy-start.10 = (bf16[512,64]{1,0:T(8,128)(2,1)}, bf16[512,64]{1,0:T(8,128)(2,1)S(1)}, u32[]{:S(2)}) copy-start(bf16[512,64]{1,0:T(8,128)(2,1)S(1)} %reshape.100) | copy-start | bytes 196612
  189.6 3.6 %copy-start.17 = (f32[2,192]{1,0:T(2,128)S(1)}, f32[2,192]{1,0:T(2,128)}, u32[]{:S(2)}) copy-start(f32[2,192]{1,0:T(2,128)} %param.28) | copy-start | bytes 4612
  218.4 4.7 %copy-start.13 = (f32[3,3072]{1,0:T(4,128)S(1)}, f32[3,3072]{1,0:T(4,128)}, u32[]{:S(2)}) copy-start(f32[3,3072]{1,0:T(4,128)} %param.23) | copy-start | bytes 110596
  218.4 14.2 %collective-permute-start = (bf16[3072,5,64]{0,2,1:T(8,128)(2,1)}, bf16[3072,5,64]{0,2,1:T(8,128)(2,1)}, u32[]{:S(2)}, u32[]{:S(2)}) collective-permute-start(bf16[3072,5,64]{0,2,1:T(8,128)(2,1)} %reshape.103), channel_id=1, source_target_pairs={{0,2},{2,0},{4,6},{6,4},{8,10},{10,8},{12,14},{14,12},{16,18},{18,... | collective-permute-start | bytes 5898248 | tf_op jit(solution)/shard_map/ppermute | solution.py:17
  223.2 6.3 %copy-start.5 = (bf16[3072,5,64]{0,2,1:T(8,128)(2,1)S(1)}, bf16[3072,5,64]{0,2,1:T(8,128)(2,1)}, u32[]{:S(2)}) copy-start(bf16[3072,5,64]{0,2,1:T(8,128)(2,1)} %reshape.103) | copy-start | bytes 5898244
  240.9 3.4 %copy-start.2 = (bf16[3072,5,64]{2,0,1:T(8,128)(2,1)}, bf16[3072,5,64]{2,0,1:T(8,128)(2,1)S(1)}, u32[]{:S(2)}) copy-start(bf16[3072,5,64]{2,0,1:T(8,128)(2,1)S(1)} %get-tuple-element.11) | copy-start | bytes 5898244
  240.9 3.5 %copy-start.3 = (bf16[3072,5,64]{2,0,1:T(8,128)(2,1)}, bf16[3072,5,64]{2,0,1:T(8,128)(2,1)S(1)}, u32[]{:S(2)}) copy-start(bf16[3072,5,64]{2,0,1:T(8,128)(2,1)S(1)} %get-tuple-element.12) | copy-start | bytes 5898244
  248.6 3.6 %copy-start.4 = (bf16[512,3072]{1,0:T(8,128)(2,1)S(1)}, bf16[512,3072]{1,0:T(8,128)(2,1)}, u32[]{:S(2)}) copy-start(bf16[512,3072]{1,0:T(8,128)(2,1)} %add_convert_fusion) | copy-start | bytes 9437188
  248.6 3.8 %copy-start.9 = (bf16[3072,2,128]{0,2,1:T(8,128)(2,1)S(1)}, bf16[3072,2,128]{0,2,1:T(8,128)(2,1)}, u32[]{:S(2)}) copy-start(bf16[3072,2,128]{0,2,1:T(8,128)(2,1)} %copy.91) | copy-start | bytes 4718596
  252.4 3.9 %copy-start.8 = (bf16[3072,2,128]{0,2,1:T(8,128)(2,1)S(1)}, bf16[3072,2,128]{0,2,1:T(8,128)(2,1)}, u32[]{:S(2)}) copy-start(bf16[3072,2,128]{0,2,1:T(8,128)(2,1)} %copy.93) | copy-start | bytes 4718596
  256.2 4.0 %copy-start.6 = (bf16[3072,512]{1,0:T(8,128)(2,1)S(1)}, bf16[3072,512]{1,0:T(8,128)(2,1)}, u32[]{:S(2)}) copy-start(bf16[3072,512]{1,0:T(8,128)(2,1)} %all-gather.3.cloned.1.call-done) | copy-start | bytes 9437188
  264.1 20.7 %copy-start.14 = (f32[3072]{0:T(1024)S(1)}, f32[3072]{0:T(1024)}, u32[]{:S(2)}) copy-start(f32[3072]{0:T(1024)} %param.31) | copy-start | bytes 36868
  264.1 10.5 %all-to-all-start.1 = ((bf16[16,16,128]{2,1,0:T(8,128)(2,1)}), bf16[16,16,128]{2,1,0:T(8,128)(2,1)S(1)}, u32[]{:S(2)}, u32[]{:S(2)}) async-start(bf16[16,16,128]{2,1,0:T(8,128)(2,1)} %bitcast.24), calls=%async_computation.1 | async-start | bytes 131072 | tf_op jit(solution)/shard_map/all_to_all | solution.py:197
  274.6 14.6 %copy-start.1 = (bf16[3,3,3,16,512]{4,3,2,1,0:T(8,128)(2,1)S(1)}, bf16[3,3,3,16,512]{4,3,2,1,0:T(8,128)(2,1)}, u32[]{:S(2)}) copy-start(bf16[3,3,3,16,512]{4,3,2,1,0:T(8,128)(2,1)} %param.19) | copy-start | bytes 1327108
  278.4 6.4 %collective-permute-start.1 = (f32[16,3072]{1,0:T(8,128)S(1)}, f32[16,3072]{1,0:T(8,128)S(1)}, u32[]{:S(2)}, u32[]{:S(2)}) collective-permute-start(f32[16,3072]{1,0:T(8,128)S(1)} %fusion.51), channel_id=1, source_target_pairs={{0,1},{1,0},{2,3},{3,2},{4,5},{5,4},{6,7},{7,6},{8,9},{9,8},{10,11... | collective-permute-start | bytes 589832 | tf_op jit(solution)/shard_map/ppermute | solution.py:212
Sparse Core Ops, SparseCore 0:
  30.8 66.3 all-gather.2
where the time goes:
time: 297 us; the launch traced here: 296 us
  blocking collectives  169 us (57%)
  matrix products  37.4 us (13%)
  local copies, waits for them, and re-layouts  29.8 us (10%)
  other arithmetic  21.1 us (7%)
  between operations  14.6 us (5%)
  waiting for transfers between devices  12.4 us (4%)
  starting transfers between devices  11.4 us (4%)
    psum x1, blocking collectives, group_norm(): sums = lax.psum(sums, ('seq', 'head'))  83.9 us
    all_gather x1, blocking collectives, all_patches(): parts = lax.all_gather(flat, ('seq', 'head'), axis=0, tiled=False)  68.1 us
    all_gather x1, blocking collectives, body(): mod = lax.all_gather(text_mod, 'seq', axis=1, tiled=True)  17.4 us
    dot_general x1, matrix products, body(): jnp.dot(text_table, chosen, preferred_element_type=jnp.float32)  9.15 us
    all_to_all x1, starting transfers between devices, body(): both = lax.all_to_all(both, 'seq', split_axis=0, concat_axis=0, tiled=True)  7.4 us
    all_to_all x1, waiting for transfers between devices, body(): lax.all_to_all(attended, 'seq', split_axis=0, concat_axis=0, tiled=True)  6.85 us
    reshape x2, local copies, waits for them, and re-layouts, body(): both = both.reshape(seq_n * depth, 5, cols)  6.84 us
    convert_element_type x1, other arithmetic, modulate(): return (normed * (1.0 + image_mod[1]) + image_mod[0]).astype(jnp.bfloat16)  6.3 us
  transfers between devices with their start and end apart: 5, of which 2 were waited for; matrix products, arithmetic and copies ran while one was open for 21% of the time, Pallas kernels for 0%

commit v1 on v0

--- a/solution.py
+++ b/solution.py
@@ -31,7 +31,7 @@
         [jnp.sum(values, axis=(0, 1, 2)), jnp.sum(values * values, axis=(0, 1, 2))]
     )
     sums = jnp.sum(chan_sums.reshape(2, GN_GROUPS, per_group), axis=2)
-    sums = lax.psum(sums, ("seq", "head"))
+    sums = lax.psum(lax.psum(sums, "head"), "seq")
     cell_count = (
         frame_count
         * row_count

time: 297 us -> 285 us (0.960)
  blocking collectives: 169 us -> 158 us
    psum x1 -> x2, blocking collectives: 83.9 us -> 63.8 us  [group_norm(): sums = lax.psum(lax.psum(sums, 'head'), 'seq')]
    all_gather x1, blocking collectives: 68.1 us -> 76.6 us  [all_patches(): parts = lax.all_gather(flat, ('seq', 'head'), axis=0, tiled=False)]
  transfers between devices with their start and end apart: 5 -> 5, of which waited for: 2 -> 2; matrix products, arithmetic and copies ran while one was open for 21% -> 22% of each run, Pallas kernels for 0% -> 0%
where the time goes in v1:
time: 285 us
  blocking collectives  158 us (55%)
  matrix products  37.4 us (13%)
  local copies, waits for them, and re-layouts  29.8 us (10%)
  other arithmetic  21.1 us (7%)
  between operations  14.6 us (5%)
  waiting for transfers between devices  12.4 us (4%)
  starting transfers between devices  11.4 us (4%)
    all_gather x1, blocking collectives, all_patches(): parts = lax.all_gather(flat, ('seq', 'head'), axis=0, tiled=False)  76.6 us
    psum x2, blocking collectives, group_norm(): sums = lax.psum(lax.psum(sums, 'head'), 'seq')  63.8 us
    all_gather x1, blocking collectives, body(): mod = lax.all_gather(text_mod, 'seq', axis=1, tiled=True)  17.4 us
    dot_general x1, matrix products, body(): jnp.dot(text_table, chosen, preferred_element_type=jnp.float32)  9.17 us
    all_to_all x1, starting transfers between devices, body(): both = lax.all_to_all(both, 'seq', split_axis=0, concat_axis=0, tiled=True)  7.4 us
    reshape x2, local copies, waits for them, and re-layouts, body(): both = both.reshape(seq_n * depth, 5, cols)  6.86 us
    all_to_all x1, waiting for transfers between devices, body(): lax.all_to_all(attended, 'seq', split_axis=0, concat_axis=0, tiled=True)  6.85 us
    convert_element_type x1, other arithmetic, modulate(): return (normed * (1.0 + image_mod[1]) + image_mod[0]).astype(jnp.bfloat16)  6.31 us
  transfers between devices with their start and end apart: 5, of which 2 were waited for; matrix products, arithmetic and copies ran while one was open for 22% of the time, Pallas kernels for 0%

profile of v1, /device:TPU:0, one launch (start us, length us, event | category | flops | bytes accessed | tf_op | source)
XLA Modules:
  0.0 284.5 jit_solution(480143218326398796)
XLA Ops:
  6.5 2.5 copy.83
  9.0 1.6 copy.82
  10.7 0.4 pad_maximum_fusion
  11.1 0.2 copy.84
  11.3 2.6 copy.85
  14.0 7.4 %all-to-all-start = ((bf16[16,192,320]{2,1,0:T(8,128)(2,1)}), bf16[16,192,320]{2,1,0:T(8,128)(2,1)}, u32[]{:S(2)}, u32[]{:S(2)}) async-start(bf16[16,192,320]{2,1,0:T(8,128)(2,1)} %copy.85), calls=%async_computation | async-start | bytes 4718592 | tf_op jit(solution)/shard_map/all_to_all | solution.py:132
  21.4 0.0 all-gather.3.cloned.1.call-start
  21.5 9.2 %fusion.23 = bf16[192,512]{1,0:T(8,128)(2,1)} fusion(bf16[192,16384]{1,0:T(8,128)(2,1)} %param.27, s32[512]{0:T(512)S(1)} %copy-done.19), kind=kOutput, calls=%fused_computation.34 | convolution fusion | flops 3229712384 | bytes 6490112 | tf_op jit(solution)/shard_map/dot_general | solution.py:139
  30.7 0.1 convert_reduce_fusion.1
  30.8 0.1 stack.10
  30.9 0.1 stack.9
  30.9 0.1 maximum_reduce_fusion
  31.0 4.9 %psum.14 = f32[2,32]{1,0:T(2,128)S(1)} all-reduce(f32[2,32]{1,0:T(2,128)S(1)} %maximum_reduce_fusion), channel_id=1, replica_groups=mesh['seq'=16,'head'=2] {'head'}, use_global_device_ids=true, to_apply=%region_3.4 | all-reduce | flops 64 | bytes 512 | tf_op jit(solution)/shard_map/psum | solution.py:34
  36.0 58.8 %psum.15 = f32[2,32]{1,0:T(2,128)S(1)} all-reduce(f32[2,32]{1,0:T(2,128)S(1)} %psum.14), channel_id=1, replica_groups=mesh['seq'=16,'head'=2] {'seq'}, use_global_device_ids=true, to_apply=%region_4.5 | all-reduce | flops 64 | bytes 512 | tf_op jit(solution)/shard_map/psum | solution.py:34
  94.8 0.1 broadcast_in_dim.15
  94.9 0.1 mul.93
  95.0 0.1 broadcast_in_dim.14
  95.0 0.1 sub.50
  95.1 0.1 fusion.50
  95.3 0.1 maximum_bitcast_fusion.2
  95.3 4.2 %convolution_reduce_fusion = f32[8,4,6,16]{3,2,1,0:T(8,128)S(1)} fusion(bf16[3,3,3,16,512]{4,3,2,1,0:T(8,128)(2,1)S(1)} %copy-done, bf16[1,10,2,4,512]{4,3,2,1,0:T(4,128)(2,1)S(1)} %maximum_bitcast_fusion.2), kind=kOutput, calls=%fused_computation.36 | convolution fusion | flops 28311552 | bytes 536576 | tf_op jit(solution)/shard_map/conv_general_dilated | solution.py:73
  99.6 0.1 all_gather_reshape_squeeze.3
  99.7 76.6 %all_gather.9 = f32[32,24,128]{2,1,0:T(8,128)S(1)} all-gather(f32[1,24,128]{2,1,0:T(8,128)S(1)} %all_gather_reshape_squeeze.3), channel_id=1, replica_groups=mesh['seq'=16,'head'=2] {'seq','head'}, dimensions={0}, use_global_device_ids=true | all-gather | bytes 405504 | tf_op jit(solution)/shard_map/all_gather | solution.py:82
  176.3 0.3 reshape.98
  176.7 0.1 slice.94
  176.8 0.1 add.181
  176.9 0.2 fusion.65
  177.1 0.1 fusion.68
  177.2 0.2 fusion.34
  177.4 0.1 reshape.99
  177.6 0.3 copy.81
  177.8 0.1 reshape.100
  178.0 3.6 %add_reduce_fusion = (f32[512]{0:T(512)S(1)}, f32[512,3072]{1,0:T(8,128)}) fusion(f32[3072]{0:T(1024)S(1)} %copy-done.11, bf16[512,64]{1,0:T(8,128)(2,1)S(1)} %reshape.100, bf16[64,3072]{1,0:T(8,128)(2,1)S(1)} %copy-done.7), kind=kOutput, calls=%fused_computation.15 | convolution fusion | flops 204471808 | bytes 6764544 | tf_op jit(solution)/shard_map/dot_general | solution.py:95
  181.7 17.4 %all-gather = f32[16,192,2]{1,2,0:T(2,128)S(1)} all-gather(f32[1,192,2]{1,2,0:T(2,128)S(1)} %bitcast.101), channel_id=1, replica_groups=mesh['seq'=16,'head'=2] {'seq'}, dimensions={0}, use_global_device_ids=true | all-gather | bytes 26112 | tf_op jit(solution)/shard_map/all_gather | solution.py:143
  199.1 0.1 reshape.110
  199.2 3.9 %copy.86 = bf16[16,192,320]{1,0,2:T(8,128)(2,1)S(1)} copy(bf16[16,192,320]{2,1,0:T(8,128)(2,1)} %all-to-all-done) | data formatting | bytes 3932160 | tf_op jit(solution)/shard_map/all_to_all | solution.py:132
  203.1 3.8 %reshape.103 = bf16[3072,5,64]{0,2,1:T(8,128)(2,1)} reshape(bf16[16,192,320]{1,0,2:T(8,128)(2,1)S(1)} %copy.86) | data formatting | bytes 3932160 | tf_op jit(solution)/shard_map/reshape | solution.py:133
  206.9 0.3 collective-permute-start
  207.2 3.7 %multiply_reduce_fusion = f32[512]{0:T(512)S(1)} fusion(f32[512,3072]{1,0:T(8,128)} %get-tuple-element.29, f32[512]{0:T(512)S(1)} %broadcast_multiply_fusion.1, f32[3072]{0:T(1024)S(1)} %copy-done.11), kind=kLoop, calls=%fused_computation.14 | loop fusion | flops 6290944 | bytes 6307840 | tf_op jit(solution)/shard_map/reduce_sum | solution.py:98
  211.7 6.3 %add_convert_fusion = bf16[512,3072]{1,0:T(8,128)(2,1)} fusion(f32[512,3072]{1,0:T(8,128)} %get-tuple-element.29, f32[3072]{0:T(1024)S(1)} %bitcast.95, f32[3072]{0:T(1024)S(1)} %bitcast.96, f32[512]{0:T(512)S(1)} %add_rsqrt_fusion.1, f32[512]{0:T(512)S(1)} %broadcast_multiply_fusion.1, f32[3072]{0:T(1024)S(1)} %copy-done.11), kind=kLoop, calls=%fused_computation.13 | loop fusion | flops 9437184 | bytes 9478144 | tf_op jit(solution)/shard_map/convert_element_type | solution.py:100
  218.0 3.1 %copy.87 = bf16[3072,5,64]{2,0,1:T(8,128)(2,1)} copy(bf16[3072,5,64]{0,2,1:T(8,128)(2,1)S(1)} %copy-done.5) | data formatting | bytes 3932160 | tf_op jit(solution)/shard_map/reshape | solution.py:133
  221.1 4.7 %copy.88 = bf16[3072,5,64]{2,0,1:T(8,128)(2,1)} copy(bf16[3072,5,64]{0,2,1:T(8,128)(2,1)} %collective-permute-done) | data formatting | bytes 3932160 | tf_op jit(solution)/shard_map/ppermute | solution.py:17
  225.8 3.6 %broadcast_select_fusion.1 = (bf16[3072,5,64]{2,0,1:T(8,128)(2,1)S(1)}, bf16[3072,5,64]{2,0,1:T(8,128)(2,1)S(1)}) fusion(bf16[3072,5,64]{2,0,1:T(8,128)(2,1)} %copy.87, bf16[3072,5,64]{2,0,1:T(8,128)(2,1)} %copy.88, pred[]{:T(512)S(6)} %eq.14), kind=kLoop, calls=%fused_computation.17 | loop fusion | flops 1966080 | bytes 7864321 | tf_op jit(solution)/shard_map/jit(_where)/select_n | solution.py:20
  229.4 3.3 %pad_maximum_fusion.2 = (bf16[3072,2,128]{2,0,1:T(8,128)(2,1)S(1)}, bf16[3072,2,128]{2,0,1:T(8,128)(2,1)}) fusion(bf16[3072,5,64]{2,0,1:T(8,128)(2,1)S(1)} %get-tuple-element.12, bf16[3072,5,64]{2,0,1:T(8,128)(2,1)S(1)} %get-tuple-element.11), kind=kLoop, calls=%fused_computation.27 | loop fusion | flops 6291456 | bytes 7077888 | tf_op jit(solution)/shard_map/slice | solution.py:135
  232.8 0.2 copy-done.3
  232.9 2.6 copy.93
  235.5 1.6 copy.91
  237.1 3.5 %fusion.27 = bf16[16,2,16,128]{3,2,1,0:T(8,128)(2,1)S(1)} fusion(bf16[16,2,16,3072]{3,2,1,0:T(8,128)(2,1)} %bitcast.80, bf16[3072,5,64]{2,0,1:T(8,128)(2,1)} %copy-done.3, bf16[3072,5,64]{2,0,1:T(8,128)(2,1)} %copy-done.2), kind=kOutput, calls=%fused_computation.42 | convolution fusion | flops 404226048 | bytes 7208960 | tf_op jit(solution)/shard_map/dot_general | solution.py:171
  240.7 0.2 copy-done.9
  240.9 1.0 convolution_convert_fusion
  241.9 0.0 all-gather.3.cloned.1.call-done
  242.0 2.8 convert_reduce_fusion
  244.8 4.0 %fusion.43 = f32[512,256]{1,0:T(8,128)S(1)} fusion(bf16[3072,256]{0,1:T(8,128)(2,1)S(1)} %bitcast.83, bf16[3072,512]{1,0:T(8,128)(2,1)} %all-gather.3.cloned.1.call-done, f32[3072]{0:T(1024)S(1)} %bitcast.99, f32[3072]{0:T(1024)S(1)} %bitcast.97, f32[512]{0:T(512)S(1)} %get-tuple-element.27, f32[512]{0:T(512)S(1)} %get-tuple-element.26), kind=kOutput, calls=%fused_computation.58 | convolution fusion | flops 814743552 | bytes 5271552 | tf_op jit(solution)/shard_map/dot_general | solution.py:153
  248.8 2.1 fusion.19
  250.9 0.4 fusion.70
  251.3 0.3 fusion.25
  251.6 1.0 fusion.24
  252.6 3.6 %all-to-all-start.1 = ((bf16[16,16,128]{2,1,0:T(8,128)(2,1)}), bf16[16,16,128]{2,1,0:T(8,128)(2,1)S(1)}, u32[]{:S(2)}, u32[]{:S(2)}) async-start(bf16[16,16,128]{2,1,0:T(8,128)(2,1)} %bitcast.24), calls=%async_computation.1 | async-start | bytes 131072 | tf_op jit(solution)/shard_map/all_to_all | solution.py:197
  256.2 6.8 %all-to-all-done.1 = bf16[16,16,128]{2,1,0:T(8,128)(2,1)S(1)} async-done(((bf16[16,16,128]{2,1,0:T(8,128)(2,1)}), bf16[16,16,128]{2,1,0:T(8,128)(2,1)S(1)}, u32[]{:S(2)}, u32[]{:S(2)}) %all-to-all-start.1) | async-done | bytes 65568 | tf_op jit(solution)/shard_map/all_to_all | solution.py:197
  263.1 3.8 %fusion.51 = f32[16,3072]{1,0:T(8,128)S(1)} fusion(bf16[1024,3072]{1,0:T(8,128)(2,1)} %param.30, bf16[2,16,1024]{2,1,0:T(8,128)(2,1)S(1)} %bitcast.89, s32[]{:T(128)S(6)} %select_n.47), kind=kOutput, calls=%fused_computation.73 | convolution fusion | flops 100663296 | bytes 6520836 | tf_op jit(solution)/shard_map/dot_general | solution.py:202
  266.9 0.9 convolution_add_fusion
  267.7 5.5 %collective-permute-done.1 = f32[16,3072]{1,0:T(8,128)S(1)} collective-permute-done((f32[16,3072]{1,0:T(8,128)S(1)}, f32[16,3072]{1,0:T(8,128)S(1)}, u32[]{:S(2)}, u32[]{:S(2)}) %collective-permute-start.1) | collective-permute-done | bytes 196640 | tf_op jit(solution)/shard_map/ppermute | solution.py:212
  273.3 3.7 %fusion.12 = bf16[16,3072]{1,0:T(8,128)(2,1)S(1)} fusion(f32[16,3072]{1,0:T(8,128)S(1)} %convolution_add_fusion, f32[16,3072]{1,0:T(8,128)S(1)} %collective-permute-done.1, bf16[1024,3072]{1,0:T(8,128)(2,1)} %param.30, f32[3072]{0:T(1024)S(1)} %copy-done.14, f32[3072]{0:T(1024)S(1)} %bitcast.94, bf16[2,16,1024]{2,1,0:T(8,128)(2,1)S(1)} %bitcast.90, ...), kind=kOutput, calls=%fused_computation.23 | convolution fusion | flops 100909056 | bytes 6840324 | tf_op jit(solution)/shard_map/dot_general | solution.py:207
  277.0 0.7 reshape.108
  (58 shorter events, 0.3 us)
Async XLA Ops:
  6.5 88.8 %copy-start = (bf16[3,3,3,16,512]{4,3,2,1,0:T(8,128)(2,1)S(1)}, bf16[3,3,3,16,512]{4,3,2,1,0:T(8,128)(2,1)}, u32[]{:S(2)}) copy-start(bf16[3,3,3,16,512]{4,3,2,1,0:T(8,128)(2,1)} %param.19) | copy-start | bytes 1327108
  11.3 10.2 %copy-start.19 = (s32[512]{0:T(512)S(1)}, s32[512]{0:T(512)}, u32[]{:S(2)}) copy-start(s32[512]{0:T(512)} %param.25) | copy-start | bytes 6148
  14.0 185.2 %all-to-all-start = ((bf16[16,192,320]{2,1,0:T(8,128)(2,1)}), bf16[16,192,320]{2,1,0:T(8,128)(2,1)}, u32[]{:S(2)}, u32[]{:S(2)}) async-start(bf16[16,192,320]{2,1,0:T(8,128)(2,1)} %copy.85), calls=%async_computation | async-start | bytes 4718592 | tf_op jit(solution)/shard_map/all_to_all | solution.py:132
  21.4 9.3 %copy-start.12 = (bf16[8,2,4,512]{3,2,1,0:T(4,128)(2,1)S(1)}, bf16[8,2,4,512]{3,2,1,0:T(4,128)(2,1)}, u32[]{:S(2)}) copy-start(bf16[8,2,4,512]{3,2,1,0:T(4,128)(2,1)} %param.16) | copy-start | bytes 196612
  21.4 73.7 %copy-start.15 = (f32[512]{0:T(512)S(1)}, f32[512]{0:T(512)}, u32[]{:S(2)}) copy-start(f32[512]{0:T(512)} %param.18) | copy-start | bytes 6148
  21.4 73.7 %copy-start.16 = (f32[512]{0:T(512)S(1)}, f32[512]{0:T(512)}, u32[]{:S(2)}) copy-start(f32[512]{0:T(512)} %param.17) | copy-start | bytes 6148
  21.4 155.4 %copy-start.18 = (f32[16]{0:T(128)S(1)}, f32[16]{0:T(128)}, u32[]{:S(2)}) copy-start(f32[16]{0:T(128)} %param.20) | copy-start | bytes 196
  21.4 220.5 %all-gather.3.cloned.1.call-start = ((), (), s32[]{:S(2)}) async-start(), calls=%async_computation.2 | async-start | bytes 3342336 | tf_op jit(solution)/shard_map/all_gather | solution.py:142
  30.7 147.3 %copy-start.7 = (bf16[64,3072]{1,0:T(8,128)(2,1)S(1)}, bf16[64,3072]{1,0:T(8,128)(2,1)}, u32[]{:S(2)}) copy-start(bf16[64,3072]{1,0:T(8,128)(2,1)} %param.21) | copy-start | bytes 1179652
  30.7 147.3 %copy-start.11 = (f32[3072]{0:T(1024)S(1)}, f32[3072]{0:T(1024)}, u32[]{:S(2)}) copy-start(f32[3072]{0:T(1024)} %param.22) | copy-start | bytes 36868
  178.0 3.6 %copy-start.10 = (bf16[512,64]{1,0:T(8,128)(2,1)}, bf16[512,64]{1,0:T(8,128)(2,1)S(1)}, u32[]{:S(2)}) copy-start(bf16[512,64]{1,0:T(8,128)(2,1)S(1)} %reshape.100) | copy-start | bytes 196612
  178.0 3.6 %copy-start.17 = (f32[2,192]{1,0:T(2,128)S(1)}, f32[2,192]{1,0:T(2,128)}, u32[]{:S(2)}) copy-start(f32[2,192]{1,0:T(2,128)} %param.28) | copy-start | bytes 4612
  206.9 4.7 %copy-start.13 = (f32[3,3072]{1,0:T(4,128)S(1)}, f32[3,3072]{1,0:T(4,128)}, u32[]{:S(2)}) copy-start(f32[3,3072]{1,0:T(4,128)} %param.23) | copy-start | bytes 110596
  206.9 14.2 %collective-permute-start = (bf16[3072,5,64]{0,2,1:T(8,128)(2,1)}, bf16[3072,5,64]{0,2,1:T(8,128)(2,1)}, u32[]{:S(2)}, u32[]{:S(2)}) collective-permute-start(bf16[3072,5,64]{0,2,1:T(8,128)(2,1)} %reshape.103), channel_id=1, source_target_pairs={{0,2},{2,0},{4,6},{6,4},{8,10},{10,8},{12,14},{14,12},{16,18},{18,... | collective-permute-start | bytes 5898248 | tf_op jit(solution)/shard_map/ppermute | solution.py:17
  211.7 6.3 %copy-start.5 = (bf16[3072,5,64]{0,2,1:T(8,128)(2,1)S(1)}, bf16[3072,5,64]{0,2,1:T(8,128)(2,1)}, u32[]{:S(2)}) copy-start(bf16[3072,5,64]{0,2,1:T(8,128)(2,1)} %reshape.103) | copy-start | bytes 5898244
  229.4 3.4 %copy-start.2 = (bf16[3072,5,64]{2,0,1:T(8,128)(2,1)}, bf16[3072,5,64]{2,0,1:T(8,128)(2,1)S(1)}, u32[]{:S(2)}) copy-start(bf16[3072,5,64]{2,0,1:T(8,128)(2,1)S(1)} %get-tuple-element.11) | copy-start | bytes 5898244
  229.4 3.5 %copy-start.3 = (bf16[3072,5,64]{2,0,1:T(8,128)(2,1)}, bf16[3072,5,64]{2,0,1:T(8,128)(2,1)S(1)}, u32[]{:S(2)}) copy-start(bf16[3072,5,64]{2,0,1:T(8,128)(2,1)S(1)} %get-tuple-element.12) | copy-start | bytes 5898244
  237.1 3.6 %copy-start.4 = (bf16[512,3072]{1,0:T(8,128)(2,1)S(1)}, bf16[512,3072]{1,0:T(8,128)(2,1)}, u32[]{:S(2)}) copy-start(bf16[512,3072]{1,0:T(8,128)(2,1)} %add_convert_fusion) | copy-start | bytes 9437188
  237.1 3.8 %copy-start.9 = (bf16[3072,2,128]{0,2,1:T(8,128)(2,1)S(1)}, bf16[3072,2,128]{0,2,1:T(8,128)(2,1)}, u32[]{:S(2)}) copy-start(bf16[3072,2,128]{0,2,1:T(8,128)(2,1)} %copy.91) | copy-start | bytes 4718596
  240.9 3.9 %copy-start.8 = (bf16[3072,2,128]{0,2,1:T(8,128)(2,1)S(1)}, bf16[3072,2,128]{0,2,1:T(8,128)(2,1)}, u32[]{:S(2)}) copy-start(bf16[3072,2,128]{0,2,1:T(8,128)(2,1)} %copy.93) | copy-start | bytes 4718596
  244.7 4.0 %copy-start.6 = (bf16[3072,512]{1,0:T(8,128)(2,1)S(1)}, bf16[3072,512]{1,0:T(8,128)(2,1)}, u32[]{:S(2)}) copy-start(bf16[3072,512]{1,0:T(8,128)(2,1)} %all-gather.3.cloned.1.call-done) | copy-start | bytes 9437188
  252.6 20.7 %copy-start.14 = (f32[3072]{0:T(1024)S(1)}, f32[3072]{0:T(1024)}, u32[]{:S(2)}) copy-start(f32[3072]{0:T(1024)} %param.31) | copy-start | bytes 36868
  252.6 10.5 %all-to-all-start.1 = ((bf16[16,16,128]{2,1,0:T(8,128)(2,1)}), bf16[16,16,128]{2,1,0:T(8,128)(2,1)S(1)}, u32[]{:S(2)}, u32[]{:S(2)}) async-start(bf16[16,16,128]{2,1,0:T(8,128)(2,1)} %bitcast.24), calls=%async_computation.1 | async-start | bytes 131072 | tf_op jit(solution)/shard_map/all_to_all | solution.py:197
  263.1 14.6 %copy-start.1 = (bf16[3,3,3,16,512]{4,3,2,1,0:T(8,128)(2,1)S(1)}, bf16[3,3,3,16,512]{4,3,2,1,0:T(8,128)(2,1)}, u32[]{:S(2)}) copy-start(bf16[3,3,3,16,512]{4,3,2,1,0:T(8,128)(2,1)} %param.19) | copy-start | bytes 1327108
  266.9 6.4 %collective-permute-start.1 = (f32[16,3072]{1,0:T(8,128)S(1)}, f32[16,3072]{1,0:T(8,128)S(1)}, u32[]{:S(2)}, u32[]{:S(2)}) collective-permute-start(f32[16,3072]{1,0:T(8,128)S(1)} %fusion.51), channel_id=1, source_target_pairs={{0,1},{1,0},{2,3},{3,2},{4,5},{5,4},{6,7},{7,6},{8,9},{9,8},{10,11... | collective-permute-start | bytes 589832 | tf_op jit(solution)/shard_map/ppermute | solution.py:212
Sparse Core Ops, SparseCore 0:
  30.8 65.9 all-gather.2
